TPU v7x, 256 devices: a whole 4x4x8 slice. The times are simulated.
256 devices in a mesh: grid: 64 (over z, y, core), lev: 4 (over x).
Axes of the slice: x: 4, y: 4, z: 8, core: 2. Of those that a mesh axis runs over, the one named last changes fastest.
Arguments:
- prior_fields: float32 [128, 8, 32768], P('grid', 'lev'), may hold values from -6 to 6
- channel_weights: float32 [8, 4], P('lev'), may hold values from 0.1 to 1
- obs_owner: int32 [4], replicated, may hold values from 0 to 63
- obs_offset: int32 [4, 4, 64], replicated, may hold values from 0 to 511
- obs_value: float32 [4, 4, 64], P(None, 'lev'), may hold values from -30 to 30
- obs_error: float32 [4, 4, 64], P(None, 'lev'), may hold values from 0.5 to 2
- ancestors: int32 [4, 4, 64, 128], P(None, 'lev', 'grid'), may hold values from 0 to 127
Outputs:
- posterior_fields: float32 [128, 8, 32768], P('grid', 'lev')
All inputs are finite; a program needn't handle non-finite values.
Results may differ from a plain program's by a relative error of at most 0.0003.
Values sent between devices are 32-bit elements; how exact they have to be, the bound alone decides.
A program may use at most 128 MiB of HBM per device.

v0:
```python
import jax
import jax.numpy as jnp
from jax import lax
from jax.sharding import PartitionSpec as P

NB = 4
HIGH = lax.Precision.HIGHEST


def spread(value, axis, source):
    kept = jnp.where(lax.axis_index(axis) == source, value, 0).astype(value.dtype)
    return lax.psum(kept, axis)


def blend_matrices(prior_obs, observed, obs_dev, centres, positions, scale, parents):
    count = observed.shape[0]
    members = prior_obs.shape[1]
    innovation = ((observed[:, None] - prior_obs) / obs_dev[:, None]) ** 2
    distance = (centres[:, None] - positions[None, :]) / scale
    taper = jnp.exp(-0.5 * distance * distance)
    log_weight = -0.5 / count * jnp.dot(taper, innovation, precision=HIGH)
    top_value = jnp.max(log_weight, axis=1, keepdims=True)
    expo_weight = jnp.exp(log_weight - top_value)
    weight = expo_weight / jnp.sum(expo_weight, axis=1, keepdims=True)
    alpha = 0.8 * (1.0 - jnp.exp(-jnp.sum(taper, axis=1) / count))
    onehot = (parents[:, :, None] == jnp.arange(members, dtype=jnp.int32)[None, None, :]).astype(
        jnp.float32
    )
    identity = jnp.eye(members, dtype=jnp.float32)
    remain = 1.0 - alpha
    return (
        alpha[:, None, None] * onehot
        + remain[:, None, None] * identity[None]
        + (weight - 1.0 / members)[:, None, :]
    )


def body(prior_fields, channel_weights, obs_owner, obs_offset, obs_value, obs_error, ancestors):
    grid_count = lax.axis_size("grid")
    member_slab, group_depth, cells = prior_fields.shape
    members = member_slab * grid_count
    block_cells = cells // grid_count
    local_regions = ancestors.shape[2]
    region_cells = block_cells // local_regions
    scale = local_regions * grid_count / 2.0
    groups = channel_weights.shape[1]
    count = obs_offset.shape[2]
    group = lax.axis_index("lev")
    block = lax.axis_index("grid")
    region_list = jnp.arange(local_regions, dtype=jnp.int32)
    centres = (block * local_regions + region_list).astype(jnp.float32) + 0.5
    first_cells = obs_offset[0].reshape(-1)
    fields = lax.all_to_all(prior_fields, "grid", split_axis=2, concat_axis=0, tiled=True)
    picked = fields[:, :, first_cells]
    for batch in range(NB):
        owner = obs_owner[batch]
        if batch > 0:
            picked = fields[:, :, obs_offset[batch].reshape(-1)]
        partial_value = jnp.einsum(
            "mlgk,lg->gkm",
            picked.reshape(members, group_depth, groups, count),
            channel_weights,
            precision=HIGH,
        )
        shared = spread(partial_value, "grid", owner)
        priors = lax.psum(shared, "lev")
        own_priors = lax.dynamic_index_in_dim(priors, group, 0, keepdims=False)
        own_offsets = lax.dynamic_index_in_dim(obs_offset[batch], group, 0, keepdims=False)
        positions = (owner * block_cells + own_offsets).astype(jnp.float32) / region_cells
        blend = blend_matrices(
            own_priors,
            obs_value[batch, 0],
            obs_error[batch, 0],
            centres,
            positions,
            scale,
            ancestors[batch, 0],
        )
        slab = fields.reshape(members, group_depth, local_regions, region_cells)
        mixed = jnp.einsum("rjm,mlrc->jlrc", blend, slab, precision=HIGH)
        fields = mixed.reshape(members, group_depth, block_cells)
    return lax.all_to_all(fields, "grid", split_axis=0, concat_axis=2, tiled=True)


def solution(mesh):
    in_specs = (
        P("grid", "lev", None),
        P("lev", None),
        P(),
        P(),
        P(None, "lev", None),
        P(None, "lev", None),
        P(None, "lev", "grid", None),
    )
    out_specs = P("grid", "lev", None)
    return jax.shard_map(body, mesh=mesh, in_specs=in_specs, out_specs=out_specs, check_vma=False)
```

profile of v0, /device:TPU:1, one launch (start us, length us, event | category | flops | bytes accessed | tf_op | source)
XLA Modules:
  0.0 1151.4 jit_solution(4428390036950253252)
XLA Ops:
  6.5 32.4 %copy.30 = f32[2,2,32768]{1,0,2:T(2,128)} copy(f32[2,2,32768]{2,1,0:T(2,128)} %param.7) | data formatting | bytes 1048576 | tf_op args[0]
  39.0 49.5 %reshape.797 = f32[64,1,2048]{2,1,0:T(1,128)} reshape(f32[32768,2,2]{2,1,0:T(2,128)} %bitcast.174) | data formatting | bytes 1048576
  88.5 13.2 %all-to-all-start = ((f32[64,1,2048]{2,1,0:T(1,128)}), f32[64,1,2048]{2,1,0:T(1,128)S(1)}, u32[]{:S(2)}, u32[]{:S(2)}) async-start(f32[64,1,2048]{2,1,0:T(1,128)} %reshape.797), calls=%async_computation | async-start | bytes 1048576 | tf_op jit(solution)/shard_map/all_to_all | solution.py:53
  103.3 16.1 %all-to-all-done = f32[64,1,2048]{2,1,0:T(1,128)S(1)} async-done(((f32[64,1,2048]{2,1,0:T(1,128)}), f32[64,1,2048]{2,1,0:T(1,128)S(1)}, u32[]{:S(2)}, u32[]{:S(2)}) %all-to-all-start) | async-done | bytes 524320 | tf_op jit(solution)/shard_map/all_to_all | solution.py:53
  119.9 1.9 reduce.32
  121.8 53.4 %reshape.798 = f32[32768,2,2]{2,1,0:T(2,128)} reshape(f32[64,2048]{1,0:T(8,128)S(1)} %reduce.32) | data formatting | bytes 1048576
  175.2 35.6 %copy.31 = f32[2,2,64,512]{3,0,2,1:T(2,128)S(1)} copy(f32[2,2,64,512]{1,0,3,2:T(2,128)} %bitcast.173) | data formatting | bytes 1048576 | tf_op jit(solution)/shard_map/all_to_all | solution.py:53
  211.5 1.0 gather_fusion
  214.0 169.1 %all-reduce.9.cloned.1.call-done = f32[4,64,128]{2,1,0:T(8,128)} async-done(((f32[4,64,128]{2,1,0:T(8,128)}), f32[4,64,128]{2,1,0:T(8,128)}) %all-reduce.9.cloned.1.call-update) | async-done | bytes 131088 | tf_op jit(solution)/shard_map/psum | solution.py:12
  385.4 41.5 %all-reduce.11.cloned.1.call-done = f32[4,64,128]{2,1,0:T(8,128)} async-done(((f32[4,64,128]{2,1,0:T(8,128)}), f32[4,64,128]{2,1,0:T(8,128)}) %all-reduce.11.cloned.1.call-update) | async-done | bytes 131088 | tf_op jit(solution)/shard_map/psum | solution.py:66
  426.9 1.6 fusion.107
  428.4 1.3 fusion.97
  429.8 1.3 divide_add_fusion.3
  432.0 1.0 gather_fusion.1
  434.5 175.3 %all-reduce.13.cloned.1.call-done = f32[4,64,128]{2,1,0:T(8,128)} async-done(((f32[4,64,128]{2,1,0:T(8,128)}), f32[4,64,128]{2,1,0:T(8,128)}) %all-reduce.13.cloned.1.call-update) | async-done | bytes 131088 | tf_op jit(solution)/shard_map/psum | solution.py:12
  612.1 41.4 %all-reduce.15.cloned.1.call-done = f32[4,64,128]{2,1,0:T(8,128)} async-done(((f32[4,64,128]{2,1,0:T(8,128)}), f32[4,64,128]{2,1,0:T(8,128)}) %all-reduce.15.cloned.1.call-update) | async-done | bytes 131088 | tf_op jit(solution)/shard_map/psum | solution.py:66
  653.5 1.6 fusion.108
  655.1 1.3 fusion.98
  656.4 1.3 divide_add_fusion.2
  657.8 1.0 convolution_bitcast_fusion.2
  662.0 175.4 %all-reduce.17.cloned.1.call-done = f32[4,64,128]{2,1,0:T(8,128)} async-done(((f32[4,64,128]{2,1,0:T(8,128)}), f32[4,64,128]{2,1,0:T(8,128)}) %all-reduce.17.cloned.1.call-update) | async-done | bytes 131088 | tf_op jit(solution)/shard_map/psum | solution.py:12
  839.4 41.5 %all-reduce.19.cloned.1.call-done = f32[4,64,128]{2,1,0:T(8,128)} async-done(((f32[4,64,128]{2,1,0:T(8,128)}), f32[4,64,128]{2,1,0:T(8,128)}) %all-reduce.19.cloned.1.call-update) | async-done | bytes 131088 | tf_op jit(solution)/shard_map/psum | solution.py:66
  880.9 1.6 fusion.109
  882.5 1.3 fusion.99
  883.9 1.3 divide_add_fusion.1
  886.3 1.0 gather_fusion.3
  888.4 176.1 %all-reduce.21.cloned.1.call-done = f32[4,64,128]{2,1,0:T(8,128)} async-done(((f32[4,64,128]{2,1,0:T(8,128)}), f32[4,64,128]{2,1,0:T(8,128)}) %all-reduce.21.cloned.1.call-update) | async-done | bytes 131088 | tf_op jit(solution)/shard_map/psum | solution.py:12
  1066.5 41.8 %all-reduce.23.cloned.1.call-done = f32[4,64,128]{2,1,0:T(8,128)} async-done(((f32[4,64,128]{2,1,0:T(8,128)}), f32[4,64,128]{2,1,0:T(8,128)}) %all-reduce.23.cloned.1.call-update) | async-done | bytes 131088 | tf_op jit(solution)/shard_map/psum | solution.py:66
  1108.3 1.6 fusion.110
  1109.9 1.3 fusion.100
  1111.2 1.3 divide_add_fusion
  1113.5 30.3 %all_to_all.36 = f32[128,2,512]{2,1,0:T(2,128)S(1)} all-to-all(f32[128,2,512]{2,1,0:T(2,128)S(1)} %copy.39), channel_id=1, replica_groups=mesh['grid'=64,'lev'=4] {'grid'}, dimensions={0} | all-to-all | bytes 1048576 | tf_op jit(solution)/shard_map/all_to_all | solution.py:82
  (69 shorter events, 14.1 us)
Async XLA Ops:
  39.0 62.8 %copy-start.1 = (s32[4,4,64]{2,1,0:T(4,128)S(1)}, s32[4,4,64]{2,1,0:T(4,128)}, u32[]{:S(2)}) copy-start(s32[4,4,64]{2,1,0:T(4,128)} %param.10) | copy-start | bytes 12292
  39.0 63.0 %copy-start.2 = (s32[4]{0:T(128)S(1)}, s32[4]{0:T(128)}, u32[]{:S(2)}) copy-start(s32[4]{0:T(128)} %param.9) | copy-start | bytes 52
  39.0 64.3 %copy-start.4 = (f32[4,1,64]{2,1,0:T(1,128)S(1)}, f32[4,1,64]{2,1,0:T(1,128)}, u32[]{:S(2)}) copy-start(f32[4,1,64]{2,1,0:T(1,128)} %param.12) | copy-start | bytes 3076
  39.0 64.3 %copy-start.5 = (f32[4,1,64]{2,1,0:T(1,128)S(1)}, f32[4,1,64]{2,1,0:T(1,128)}, u32[]{:S(2)}) copy-start(f32[4,1,64]{2,1,0:T(1,128)} %param.11) | copy-start | bytes 3076
  88.5 30.9 %all-to-all-start = ((f32[64,1,2048]{2,1,0:T(1,128)}), f32[64,1,2048]{2,1,0:T(1,128)S(1)}, u32[]{:S(2)}, u32[]{:S(2)}) async-start(f32[64,1,2048]{2,1,0:T(1,128)} %reshape.797), calls=%async_computation | async-start | bytes 1048576 | tf_op jit(solution)/shard_map/all_to_all | solution.py:53
  101.7 281.4 %all-reduce.9.cloned.1.call-start = ((), (), s32[]{:S(2)}) async-start(), calls=%async_computation.2 | async-start | bytes 262144 | tf_op jit(solution)/shard_map/psum | solution.py:12
  175.2 37.3 %copy-start = (f32[2,4]{1,0:T(2,128)S(1)}, f32[2,4]{1,0:T(2,128)}, u32[]{:S(2)}) copy-start(f32[2,4]{1,0:T(2,128)} %param.8) | copy-start | bytes 100
  175.2 38.1 %copy-start.3 = (s32[4,1,1,128]{3,2,1,0:T(1,128)S(1)}, s32[4,1,1,128]{3,2,1,0:T(1,128)}, u32[]{:S(2)}) copy-start(s32[4,1,1,128]{3,2,1,0:T(1,128)} %param.13) | copy-start | bytes 6148
  213.3 213.6 %all-reduce.11.cloned.1.call-start = ((), (), s32[]{:S(2)}) async-start(), calls=%async_computation.3 | async-start | bytes 262144 | tf_op jit(solution)/shard_map/psum | solution.py:66
  383.1 226.7 %all-reduce.13.cloned.1.call-start = ((), (), s32[]{:S(2)}) async-start(), calls=%async_computation.4 | async-start | bytes 262144 | tf_op jit(solution)/shard_map/psum | solution.py:12
  433.8 219.7 %all-reduce.15.cloned.1.call-start = ((), (), s32[]{:S(2)}) async-start(), calls=%async_computation.5 | async-start | bytes 262144 | tf_op jit(solution)/shard_map/psum | solution.py:66
  609.8 227.5 %all-reduce.17.cloned.1.call-start = ((), (), s32[]{:S(2)}) async-start(), calls=%async_computation.6 | async-start | bytes 262144 | tf_op jit(solution)/shard_map/psum | solution.py:12
  661.3 219.6 %all-reduce.19.cloned.1.call-start = ((), (), s32[]{:S(2)}) async-start(), calls=%async_computation.7 | async-start | bytes 262144 | tf_op jit(solution)/shard_map/psum | solution.py:66
  837.4 227.1 %all-reduce.21.cloned.1.call-start = ((), (), s32[]{:S(2)}) async-start(), calls=%async_computation.8 | async-start | bytes 262144 | tf_op jit(solution)/shard_map/psum | solution.py:12
  888.3 220.0 %all-reduce.23.cloned.1.call-start = ((), (), s32[]{:S(2)}) async-start(), calls=%async_computation.9 | async-start | bytes 262144 | tf_op jit(solution)/shard_map/psum | solution.py:66
Sparse Core Ops, SparseCore 0:
  213.4 169.6 all-reduce.8
  385.4 41.3 all-reduce.10
  433.9 175.8 all-reduce.12
  612.1 41.3 all-reduce.14
  661.4 175.8 all-reduce.16
  839.5 41.3 all-reduce.18
  888.5 175.9 all-reduce.20
  1066.9 41.3 all-reduce.22
where the time goes:
time: 1160 us; the launch traced here: 1150 us
  waiting for transfers between devices  878 us (76%)
  local copies, waits for them, and re-layouts  179 us (15%)
  blocking collectives  30.3 us (3%)
  between operations  21.8 us (2%)
  other arithmetic  18.7 us (2%)
  starting transfers between devices  13.7 us (1%)
    psum x4, waiting for transfers between devices, spread(): return lax.psum(kept, axis)  696 us
    psum x4, waiting for transfers between devices, body(): priors = lax.psum(shared, 'lev')  166 us
    unnamed x18, local copies, waits for them, and re-layouts  136 us
    all_to_all x4, local copies, waits for them, and re-layouts, body(): lax.all_to_all(prior_fields, 'grid', split_axis=2, concat_axis=0, tiled=T...  36.7 us
    all_to_all x1, blocking collectives, body(): lax.all_to_all(fields, 'grid', split_axis=0, concat_axis=2, tiled=True)  30.3 us
  transfers between devices with their start and end apart: 9, of which 9 were waited for; matrix products, arithmetic and copies ran while one was open for 0% of the time, Pallas kernels for 0%

commit v1 on v0

--- a/solution.py
+++ b/solution.py
@@ -5,11 +5,12 @@
 
 NB = 4
 HIGH = lax.Precision.HIGHEST
+set_block = lambda arr_in, chip_axis: lax.all_gather(arr_in, chip_axis).sum(axis=0)
 
 
 def spread(value, axis, source):
     kept = jnp.where(lax.axis_index(axis) == source, value, 0).astype(value.dtype)
-    return lax.psum(kept, axis)
+    return set_block(kept, axis)
 
 
 def blend_matrices(prior_obs, observed, obs_dev, centres, positions, scale, parents):

time: 1160 us -> 804 us (0.69)
  waiting for transfers between devices: 878 us -> 509 us
  other arithmetic: 18.7 us -> 36.8 us
    psum x4 -> x0, waiting for transfers between devices: 696 us -> none  [spread(): return lax.psum(kept, axis)]
    all_gather x0 -> x4, waiting for transfers between devices: none -> 336 us  [lax.all_gather(arr_in, chip_axis).sum(axis=0)]
    reduce_sum x0 -> x4, other arithmetic: none -> 18.1 us  [lax.all_gather(arr_in, chip_axis).sum(axis=0)]
where the time goes in v1:
time: 804 us; the launch traced here: 800 us
  waiting for transfers between devices  509 us (63%)
  local copies, waits for them, and re-layouts  179 us (22%)
  other arithmetic  36.8 us (5%)
  blocking collectives  30.3 us (4%)
  between operations  21.4 us (3%)
  starting transfers between devices  13.7 us (2%)
  matrix products  9.31 us (1%)
    all_gather x4, waiting for transfers between devices, lax.all_gather(arr_in, chip_axis).sum(axis=0)  336 us
    psum x4, waiting for transfers between devices, body(): priors = lax.psum(shared, 'lev')  157 us
    unnamed x18, local copies, waits for them, and re-layouts  136 us
    all_to_all x4, local copies, waits for them, and re-layouts, body(): lax.all_to_all(prior_fields, 'grid', split_axis=2, concat_axis=0, tiled=T...  36.8 us
    all_to_all x1, blocking collectives, body(): lax.all_to_all(fields, 'grid', split_axis=0, concat_axis=2, tiled=True)  30.3 us
    reduce_sum x4, other arithmetic, lax.all_gather(arr_in, chip_axis).sum(axis=0)  18.1 us
    all_to_all x1, waiting for transfers between devices, body(): lax.all_to_all(prior_fields, 'grid', split_axis=2, concat_axis=0, tiled=T...  16.2 us
  transfers between devices with their start and end apart: 9, of which 9 were waited for; matrix products, arithmetic and copies ran while one was open for 0% of the time, Pallas kernels for 0%

profile of v1, /device:TPU:1, one launch (start us, length us, event | category | flops | bytes accessed | tf_op | source)
XLA Modules:
  0.0 800.0 jit_solution(13077704125849972402)
XLA Ops:
  6.5 32.4 %copy.30 = f32[2,2,32768]{1,0,2:T(2,128)} copy(f32[2,2,32768]{2,1,0:T(2,128)} %param.7) | data formatting | bytes 1048576 | tf_op args[0]
  39.0 49.5 %reshape.801 = f32[64,1,2048]{2,1,0:T(1,128)} reshape(f32[32768,2,2]{2,1,0:T(2,128)} %bitcast.178) | data formatting | bytes 1048576
  88.5 13.2 %all-to-all-start = ((f32[64,1,2048]{2,1,0:T(1,128)}), f32[64,1,2048]{2,1,0:T(1,128)S(1)}, u32[]{:S(2)}, u32[]{:S(2)}) async-start(f32[64,1,2048]{2,1,0:T(1,128)} %reshape.801), calls=%async_computation | async-start | bytes 1048576 | tf_op jit(solution)/shard_map/all_to_all | solution.py:54
  103.2 16.2 %all-to-all-done = f32[64,1,2048]{2,1,0:T(1,128)S(1)} async-done(((f32[64,1,2048]{2,1,0:T(1,128)}), f32[64,1,2048]{2,1,0:T(1,128)S(1)}, u32[]{:S(2)}, u32[]{:S(2)}) %all-to-all-start) | async-done | bytes 524320 | tf_op jit(solution)/shard_map/all_to_all | solution.py:54
  119.9 1.9 reduce.32
  121.8 53.4 %reshape.802 = f32[32768,2,2]{2,1,0:T(2,128)} reshape(f32[64,2048]{1,0:T(8,128)S(1)} %reduce.32) | data formatting | bytes 1048576
  175.2 35.7 %copy.31 = f32[2,2,64,512]{3,0,2,1:T(2,128)S(1)} copy(f32[2,2,64,512]{1,0,3,2:T(2,128)} %bitcast.177) | data formatting | bytes 1048576 | tf_op jit(solution)/shard_map/all_to_all | solution.py:54
  214.0 79.3 %all-gather.9.cloned.1.call-done = f32[256,64,128]{2,1,0:T(8,128)} async-done(((f32[4,64,128]{2,1,0:T(8,128)}), f32[256,64,128]{2,1,0:T(8,128)}) %all-gather.9.cloned.1.call-update) | async-done | bytes 8388624 | tf_op jit(solution)/shard_map/all_gather | solution.py:8
  293.3 4.5 reduce_sum.109
  299.8 39.2 %all-reduce.5.cloned.1.call-done = f32[4,64,128]{2,1,0:T(8,128)} async-done(((f32[4,64,128]{2,1,0:T(8,128)}), f32[4,64,128]{2,1,0:T(8,128)}) %all-reduce.5.cloned.1.call-update) | async-done | bytes 131088 | tf_op jit(solution)/shard_map/psum | solution.py:67
  339.0 1.6 fusion.107
  340.6 1.3 fusion.97
  341.9 1.3 divide_add_fusion.3
  347.0 85.1 %all-gather.11.cloned.1.call-done = f32[256,64,128]{2,1,0:T(8,128)} async-done(((f32[4,64,128]{2,1,0:T(8,128)}), f32[256,64,128]{2,1,0:T(8,128)}) %all-gather.11.cloned.1.call-update) | async-done | bytes 8388624 | tf_op jit(solution)/shard_map/all_gather | solution.py:8
  432.1 4.5 reduce_sum.112
  438.6 39.2 %all-reduce.7.cloned.1.call-done = f32[4,64,128]{2,1,0:T(8,128)} async-done(((f32[4,64,128]{2,1,0:T(8,128)}), f32[4,64,128]{2,1,0:T(8,128)}) %all-reduce.7.cloned.1.call-update) | async-done | bytes 131088 | tf_op jit(solution)/shard_map/psum | solution.py:67
  477.9 1.6 fusion.108
  479.4 1.3 fusion.98
  480.8 1.3 divide_add_fusion.2
  486.3 85.5 %all-gather.13.cloned.1.call-done = f32[256,64,128]{2,1,0:T(8,128)} async-done(((f32[4,64,128]{2,1,0:T(8,128)}), f32[256,64,128]{2,1,0:T(8,128)}) %all-gather.13.cloned.1.call-update) | async-done | bytes 8388624 | tf_op jit(solution)/shard_map/all_gather | solution.py:8
  571.8 4.5 reduce_sum.115
  578.3 39.2 %all-reduce.9.cloned.1.call-done = f32[4,64,128]{2,1,0:T(8,128)} async-done(((f32[4,64,128]{2,1,0:T(8,128)}), f32[4,64,128]{2,1,0:T(8,128)}) %all-reduce.9.cloned.1.call-update) | async-done | bytes 131088 | tf_op jit(solution)/shard_map/psum | solution.py:67
  617.6 1.6 fusion.109
  619.1 1.3 fusion.99
  620.5 1.3 divide_add_fusion.1
  625.0 86.1 %all-gather.15.cloned.1.call-done = f32[256,64,128]{2,1,0:T(8,128)} async-done(((f32[4,64,128]{2,1,0:T(8,128)}), f32[256,64,128]{2,1,0:T(8,128)}) %all-gather.15.cloned.1.call-update) | async-done | bytes 8388624 | tf_op jit(solution)/shard_map/all_gather | solution.py:8
  711.1 4.5 reduce_sum.118
  717.6 39.3 %all-reduce.11.cloned.1.call-done = f32[4,64,128]{2,1,0:T(8,128)} async-done(((f32[4,64,128]{2,1,0:T(8,128)}), f32[4,64,128]{2,1,0:T(8,128)}) %all-reduce.11.cloned.1.call-update) | async-done | bytes 131088 | tf_op jit(solution)/shard_map/psum | solution.py:67
  756.9 1.6 fusion.110
  758.5 1.3 fusion.100
  759.8 1.3 divide_add_fusion
  762.0 30.3 %all_to_all.36 = f32[128,2,512]{2,1,0:T(2,128)S(1)} all-to-all(f32[128,2,512]{2,1,0:T(2,128)S(1)} %copy.39), channel_id=1, replica_groups=mesh['grid'=64,'lev'=4] {'grid'}, dimensions={0} | all-to-all | bytes 1048576 | tf_op jit(solution)/shard_map/all_to_all | solution.py:83
  (73 shorter events, 18.0 us)
Async XLA Ops:
  39.0 62.7 %copy-start.1 = (s32[4,4,64]{2,1,0:T(4,128)S(1)}, s32[4,4,64]{2,1,0:T(4,128)}, u32[]{:S(2)}) copy-start(s32[4,4,64]{2,1,0:T(4,128)} %param.10) | copy-start | bytes 12292
  39.0 62.9 %copy-start.2 = (s32[4]{0:T(128)S(1)}, s32[4]{0:T(128)}, u32[]{:S(2)}) copy-start(s32[4]{0:T(128)} %param.9) | copy-start | bytes 52
  88.5 30.9 %all-to-all-start = ((f32[64,1,2048]{2,1,0:T(1,128)}), f32[64,1,2048]{2,1,0:T(1,128)S(1)}, u32[]{:S(2)}, u32[]{:S(2)}) async-start(f32[64,1,2048]{2,1,0:T(1,128)} %reshape.801), calls=%async_computation | async-start | bytes 1048576 | tf_op jit(solution)/shard_map/all_to_all | solution.py:54
  101.7 191.6 %all-gather.9.cloned.1.call-start = ((), (), s32[]{:S(2)}) async-start(), calls=%async_computation.6 | async-start | bytes 8519680 | tf_op jit(solution)/shard_map/all_gather | solution.py:8
  175.2 37.3 %copy-start = (f32[2,4]{1,0:T(2,128)S(1)}, f32[2,4]{1,0:T(2,128)}, u32[]{:S(2)}) copy-start(f32[2,4]{1,0:T(2,128)} %param.8) | copy-start | bytes 100
  175.2 38.8 %copy-start.3 = (s32[4,1,1,128]{3,2,1,0:T(1,128)S(1)}, s32[4,1,1,128]{3,2,1,0:T(1,128)}, u32[]{:S(2)}) copy-start(s32[4,1,1,128]{3,2,1,0:T(1,128)} %param.13) | copy-start | bytes 6148
  175.2 38.8 %copy-start.4 = (f32[4,1,64]{2,1,0:T(1,128)S(1)}, f32[4,1,64]{2,1,0:T(1,128)}, u32[]{:S(2)}) copy-start(f32[4,1,64]{2,1,0:T(1,128)} %param.12) | copy-start | bytes 3076
  175.2 38.8 %copy-start.5 = (f32[4,1,64]{2,1,0:T(1,128)S(1)}, f32[4,1,64]{2,1,0:T(1,128)}, u32[]{:S(2)}) copy-start(f32[4,1,64]{2,1,0:T(1,128)} %param.11) | copy-start | bytes 3076
  213.3 125.7 %all-reduce.5.cloned.1.call-start = ((), (), s32[]{:S(2)}) async-start(), calls=%async_computation.2 | async-start | bytes 262144 | tf_op jit(solution)/shard_map/psum | solution.py:67
  297.8 134.3 %all-gather.11.cloned.1.call-start = ((), (), s32[]{:S(2)}) async-start(), calls=%async_computation.7 | async-start | bytes 8519680 | tf_op jit(solution)/shard_map/all_gather | solution.py:8
  345.9 131.9 %all-reduce.7.cloned.1.call-start = ((), (), s32[]{:S(2)}) async-start(), calls=%async_computation.3 | async-start | bytes 262144 | tf_op jit(solution)/shard_map/psum | solution.py:67
  436.6 135.2 %all-gather.13.cloned.1.call-start = ((), (), s32[]{:S(2)}) async-start(), calls=%async_computation.8 | async-start | bytes 8519680 | tf_op jit(solution)/shard_map/all_gather | solution.py:8
  485.6 131.9 %all-reduce.9.cloned.1.call-start = ((), (), s32[]{:S(2)}) async-start(), calls=%async_computation.4 | async-start | bytes 262144 | tf_op jit(solution)/shard_map/psum | solution.py:67
  576.4 134.8 %all-gather.15.cloned.1.call-start = ((), (), s32[]{:S(2)}) async-start(), calls=%async_computation.9 | async-start | bytes 8519680 | tf_op jit(solution)/shard_map/all_gather | solution.py:8
  625.0 131.9 %all-reduce.11.cloned.1.call-start = ((), (), s32[]{:S(2)}) async-start(), calls=%async_computation.5 | async-start | bytes 262144 | tf_op jit(solution)/shard_map/psum | solution.py:67
Sparse Core Ops, SparseCore 0:
  213.4 79.8 all-gather.8
  297.9 41.0 all-reduce.4
  346.1 85.9 all-gather.10
  436.8 41.0 all-reduce.6
  485.8 85.9 all-gather.12
  576.5 41.0 all-reduce.8
  625.1 85.9 all-gather.14
  715.8 41.0 all-reduce.10
